TPU v7x, 256 devices: a whole 4x4x8 slice. The times are simulated.
256 devices in a mesh: peer: 8 (over x, y_hi), space: 32 (over y_lo, z, core).
Axes of the slice: x: 4, y: 4 (y_hi: 2, y_lo: 2; y = y_hi * 2 + y_lo), z: 8, core: 2. Of those that a mesh axis runs over, the one named last changes fastest.
Arguments:
- images: bfloat16 [8, 512, 32, 512], P('peer', 'space'), may hold values from -6 to 6
- task_grad: bfloat16 [8, 512, 32, 512], P('peer', 'space'), may hold values from -6 to 6
- pairing: int32 [8], replicated, may hold values from 0 to 7, as said below
- first_kernel: bfloat16 [8, 3, 3, 512, 512], P('peer'), may hold values from -0.09375 to 0.09375
- first_scale: float32 [8, 512], P('peer'), may hold values from 0.25 to 1.75
- first_shift: float32 [8, 512], P('peer'), may hold values from -3 to 3
- second_kernel: bfloat16 [8, 3, 3, 512, 512], P('peer'), may hold values from -0.09375 to 0.09375
- second_scale: float32 [8, 512], P('peer'), may hold values from 0.25 to 1.75
- second_shift: float32 [8, 512], P('peer'), may hold values from -3 to 3
Outputs:
- input_grad: bfloat16 [8, 512, 32, 512], P('peer', 'space')
Inputs may be any that keep to these rules, and one draw needn't show every extreme that they name: `pairing`: every network index appears exactly once.
All inputs are finite; a program needn't handle non-finite values.
Results may differ from a plain program's by a relative error of at most 0.012.
Values may be sent and summed in bfloat16 or wider, within the bound.
A program may use at most 64 MiB of HBM per device.

v0:
```python
import jax
import jax.numpy as jnp
from jax import lax
from jax.sharding import PartitionSpec as P


def extended(cells, sides, width):
    for axis, dim in sides:
        count = lax.axis_size(axis)
        ends = count - 1
        head = lax.slice_in_dim(cells, 0, width, axis=dim)
        tail = lax.slice_in_dim(cells, cells.shape[dim] - width, cells.shape[dim], axis=dim)
        cells = jnp.concatenate(
            [
                lax.ppermute(tail, axis, [(i, (i + 1) % count) for i in range(ends)]),
                cells,
                lax.ppermute(head, axis, [((i + 1) % count, i) for i in range(ends)]),
            ],
            axis=dim,
        )
    return cells


def apply_dilated_filter(
    padded_row_count, filter_kernel, dilation_rate, output_rows, reverse_kernel
):
    input_width = padded_row_count.shape[1]
    padded_input = jnp.pad(padded_row_count, ((0, 0), (dilation_rate, dilation_rate), (0, 0)))
    total = jnp.zeros((output_rows, input_width, filter_kernel.shape[2]), jnp.float32)
    for kernel_tap_row in range(3):
        for kernel_tap_column in range(3):
            input_window = padded_input[
                kernel_tap_row * dilation_rate : kernel_tap_row * dilation_rate + output_rows,
                kernel_tap_column * dilation_rate : kernel_tap_column * dilation_rate + input_width,
            ]
            if reverse_kernel:
                total = total + jnp.einsum(
                    "rwo,io->rwi",
                    input_window,
                    filter_kernel[2 - kernel_tap_row, 2 - kernel_tap_column],
                    preferred_element_type=jnp.float32,
                )
            else:
                total = total + jnp.einsum(
                    "rwi,io->rwo",
                    input_window,
                    filter_kernel[kernel_tap_row, kernel_tap_column],
                    preferred_element_type=jnp.float32,
                )
    return total


def silu_slope(value):
    sig = jax.nn.sigmoid(value)
    return sig * (1.0 + value * (1.0 - sig))


def per_device(
    images,
    task_grad,
    pairing,
    first_kernel,
    first_scale,
    first_shift,
    second_kernel,
    second_scale,
    second_shift,
):
    image = images[0]
    strip_rows = image.shape[0]
    kernel_one = first_kernel[0]
    kernel_two = second_kernel[0]
    scale_one = first_scale[0]
    shift_one = first_shift[0]
    scale_two = second_scale[0]
    shift_two = second_shift[0]
    image_ext = extended(image, (("space", 0),), 2)
    pre_first = (
        scale_one * apply_dilated_filter(image_ext, kernel_one, 2, strip_rows, False) + shift_one
    )
    hidden = jax.nn.silu(pre_first).astype(jnp.bfloat16)
    hidden_ext = extended(hidden, (("space", 0),), 4)
    pre_second = (
        scale_two * apply_dilated_filter(hidden_ext, kernel_two, 4, strip_rows, False) + shift_two
    )
    feat = jax.nn.silu(pre_second).astype(jnp.bfloat16)
    partner = pairing[lax.axis_index("peer")]
    piece = lax.all_gather(feat[None], "peer", axis=0, tiled=True)
    owners = jnp.arange(piece.shape[0], dtype=jnp.int32)
    pick = (owners == partner).astype(jnp.bfloat16)
    partner_feat = jnp.einsum("k,krwc->rwc", pick, piece, preferred_element_type=jnp.float32)
    cot = task_grad[0].astype(jnp.float32) + feat.astype(jnp.float32) - partner_feat
    grad_second = (cot * silu_slope(pre_second) * scale_two).astype(jnp.bfloat16)
    grad_second_ext = extended(grad_second, (("space", 0),), 4)
    grad_hidden = apply_dilated_filter(grad_second_ext, kernel_two, 4, strip_rows, True)
    grad_first = (grad_hidden * silu_slope(pre_first) * scale_one).astype(jnp.bfloat16)
    grad_first_ext = extended(grad_first, (("space", 0),), 2)
    input_grad = apply_dilated_filter(grad_first_ext, kernel_one, 2, strip_rows, True).astype(
        jnp.bfloat16
    )
    return input_grad[None]


def solution(mesh):
    placed = (
        P("peer", "space", None, None),
        P("peer", "space", None, None),
        P(),
        P("peer", None, None, None, None),
        P("peer", None),
        P("peer", None),
        P("peer", None, None, None, None),
        P("peer", None),
        P("peer", None),
    )
    return jax.shard_map(
        per_device,
        mesh=mesh,
        in_specs=placed,
        out_specs=P("peer", "space", None, None),
        check_vma=False,
    )
```

profile of v0, /device:TPU:97, one launch (start us, length us, event | category | flops | bytes accessed | tf_op | source)
XLA Modules:
  0.0 163.8 jit_solution(12028353491544414029)
XLA Ops:
  6.5 1.0 slice_bitcast_fusion.55
  7.6 5.4 %collective-permute-start = (bf16[2,32,512]{2,1,0:T(8,128)(2,1)S(1)}, bf16[2,32,512]{2,1,0:T(8,128)(2,1)S(1)}, u32[]{:S(2)}, u32[]{:S(2)}) collective-permute-start(bf16[2,32,512]{2,1,0:T(8,128)(2,1)S(1)} %get-tuple-element.11), channel_id=1, source_target_pairs={{0,1},{1,2},{2,3},{3,4},{4,5},{5,6},{6,7},{7,8},{8,9},{9,10},{10,1... | collective-permute-start | bytes 196616 | tf_op jit(solution)/shard_map/ppermute | solution.py:15
  13.0 1.9 %collective-permute-start.1 = (bf16[2,32,512]{2,1,0:T(8,128)(2,1)S(1)}, bf16[2,32,512]{2,1,0:T(8,128)(2,1)S(1)}, u32[]{:S(2)}, u32[]{:S(2)}) collective-permute-start(bf16[2,32,512]{2,1,0:T(8,128)(2,1)S(1)} %get-tuple-element.12), channel_id=1, source_target_pairs={{1,0},{2,1},{3,2},{4,3},{5,4},{6,5},{7,6},{8,7},{9,8},{10,9},{11,1... | collective-permute-start | bytes 196616 | tf_op jit(solution)/shard_map/ppermute | solution.py:17
  15.0 4.9 %collective-permute-done.1 = bf16[2,32,512]{2,1,0:T(8,128)(2,1)S(1)} collective-permute-done((bf16[2,32,512]{2,1,0:T(8,128)(2,1)S(1)}, bf16[2,32,512]{2,1,0:T(8,128)(2,1)S(1)}, u32[]{:S(2)}, u32[]{:S(2)}) %collective-permute-start.1) | collective-permute-done | bytes 65568 | tf_op jit(solution)/shard_map/ppermute | solution.py:17
  19.8 1.4 fusion.30
  21.2 1.5 fusion.80
  22.7 1.6 fusion.45
  27.1 0.7 multiply_convert_fusion.1
  27.8 2.1 %collective-permute-start.2 = (bf16[4,32,512]{2,1,0:T(8,128)(2,1)S(1)}, bf16[4,32,512]{2,1,0:T(8,128)(2,1)S(1)}, u32[]{:S(2)}, u32[]{:S(2)}) collective-permute-start(bf16[4,32,512]{2,1,0:T(8,128)(2,1)S(1)} %get-tuple-element.9), channel_id=1, source_target_pairs={{0,1},{1,2},{2,3},{3,4},{4,5},{5,6},{6,7},{7,8},{8,9},{9,10},{10,1... | collective-permute-start | bytes 393224 | tf_op jit(solution)/shard_map/ppermute | solution.py:15
  29.9 2.4 %collective-permute-start.3 = (bf16[4,32,512]{2,1,0:T(8,128)(2,1)S(1)}, bf16[4,32,512]{2,1,0:T(8,128)(2,1)S(1)}, u32[]{:S(2)}, u32[]{:S(2)}) collective-permute-start(bf16[4,32,512]{2,1,0:T(8,128)(2,1)S(1)} %get-tuple-element.10), channel_id=1, source_target_pairs={{1,0},{2,1},{3,2},{4,3},{5,4},{6,5},{7,6},{8,7},{9,8},{10,9},{11,1... | collective-permute-start | bytes 393224 | tf_op jit(solution)/shard_map/ppermute | solution.py:17
  32.3 5.1 %collective-permute-done.3 = bf16[4,32,512]{2,1,0:T(8,128)(2,1)S(1)} collective-permute-done((bf16[4,32,512]{2,1,0:T(8,128)(2,1)S(1)}, bf16[4,32,512]{2,1,0:T(8,128)(2,1)S(1)}, u32[]{:S(2)}, u32[]{:S(2)}) %collective-permute-start.3) | collective-permute-done | bytes 131104 | tf_op jit(solution)/shard_map/ppermute | solution.py:17
  41.4 1.5 multiply_convert_fusion
  43.0 0.6 dynamic_slice.3
  43.5 74.3 %all-gather.3.cloned.1.call-done = bf16[128,32,512]{2,1,0:T(8,128)(2,1)} async-done(((bf16[16,32,512]{2,1,0:T(8,128)(2,1)}), bf16[128,32,512]{2,1,0:T(8,128)(2,1)}) %all-gather.3.cloned.1.call-update) | async-done | bytes 4194320 | tf_op jit(solution)/shard_map/all_gather | solution.py:88
  117.9 5.9 %fusion = f32[1,16,32,512]{3,0,2,1:T(1,128)S(1)} fusion(bf16[8,16,32,512]{3,2,1,0:T(8,128)(2,1)} %bitcast.184, s32[]{:T(128)} %bitcast.46), kind=kOutput, calls=%fused_computation | convolution fusion | flops 4194312 | bytes 5242884 | tf_op jit(solution)/shard_map/k,krwc->rwc/dot_general | solution.py:91
  123.8 0.6 fusion.20
  124.4 5.7 %collective-permute-start.4 = (bf16[4,32,512]{2,1,0:T(8,128)(2,1)S(1)}, bf16[4,32,512]{2,1,0:T(8,128)(2,1)S(1)}, u32[]{:S(2)}, u32[]{:S(2)}) collective-permute-start(bf16[4,32,512]{2,1,0:T(8,128)(2,1)S(1)} %get-tuple-element.7), channel_id=1, source_target_pairs={{0,1},{1,2},{2,3},{3,4},{4,5},{5,6},{6,7},{7,8},{8,9},{9,10},{10,1... | collective-permute-start | bytes 393224 | tf_op jit(solution)/shard_map/ppermute | solution.py:15
  130.0 2.1 %collective-permute-start.5 = (bf16[4,32,512]{2,1,0:T(8,128)(2,1)S(1)}, bf16[4,32,512]{2,1,0:T(8,128)(2,1)S(1)}, u32[]{:S(2)}, u32[]{:S(2)}) collective-permute-start(bf16[4,32,512]{2,1,0:T(8,128)(2,1)S(1)} %get-tuple-element.8), channel_id=1, source_target_pairs={{1,0},{2,1},{3,2},{4,3},{5,4},{6,5},{7,6},{8,7},{9,8},{10,9},{11,1... | collective-permute-start | bytes 393224 | tf_op jit(solution)/shard_map/ppermute | solution.py:17
  132.2 5.4 %collective-permute-done.5 = bf16[4,32,512]{2,1,0:T(8,128)(2,1)S(1)} collective-permute-done((bf16[4,32,512]{2,1,0:T(8,128)(2,1)S(1)}, bf16[4,32,512]{2,1,0:T(8,128)(2,1)S(1)}, u32[]{:S(2)}, u32[]{:S(2)}) %collective-permute-start.5) | collective-permute-done | bytes 131104 | tf_op jit(solution)/shard_map/ppermute | solution.py:17
  141.9 0.7 fusion.15
  142.6 2.1 %collective-permute-start.6 = (bf16[2,32,512]{2,1,0:T(8,128)(2,1)S(1)}, bf16[2,32,512]{2,1,0:T(8,128)(2,1)S(1)}, u32[]{:S(2)}, u32[]{:S(2)}) collective-permute-start(bf16[2,32,512]{2,1,0:T(8,128)(2,1)S(1)} %get-tuple-element.5), channel_id=1, source_target_pairs={{0,1},{1,2},{2,3},{3,4},{4,5},{5,6},{6,7},{7,8},{8,9},{9,10},{10,1... | collective-permute-start | bytes 196616 | tf_op jit(solution)/shard_map/ppermute | solution.py:15
  144.7 2.4 %collective-permute-start.7 = (bf16[2,32,512]{2,1,0:T(8,128)(2,1)S(1)}, bf16[2,32,512]{2,1,0:T(8,128)(2,1)S(1)}, u32[]{:S(2)}, u32[]{:S(2)}) collective-permute-start(bf16[2,32,512]{2,1,0:T(8,128)(2,1)S(1)} %get-tuple-element.6), channel_id=1, source_target_pairs={{1,0},{2,1},{3,2},{4,3},{5,4},{6,5},{7,6},{8,7},{9,8},{10,9},{11,1... | collective-permute-start | bytes 196616 | tf_op jit(solution)/shard_map/ppermute | solution.py:17
  147.1 4.4 %collective-permute-done.7 = bf16[2,32,512]{2,1,0:T(8,128)(2,1)S(1)} collective-permute-done((bf16[2,32,512]{2,1,0:T(8,128)(2,1)S(1)}, bf16[2,32,512]{2,1,0:T(8,128)(2,1)S(1)}, u32[]{:S(2)}, u32[]{:S(2)}) %collective-permute-start.7) | collective-permute-done | bytes 65568 | tf_op jit(solution)/shard_map/ppermute | solution.py:17
  155.7 1.3 fusion.16
  (73 shorter events, 15.1 us)
Async XLA Ops:
  6.5 111.3 %all-gather.3.cloned.1.call-start = ((), (), s32[]{:S(2)}) async-start(), calls=%async_computation | async-start | bytes 4718592 | tf_op jit(solution)/shard_map/all_gather | solution.py:88
  6.5 17.8 %copy-start = (bf16[1,3,3,512,512]{4,3,2,1,0:T(8,128)(2,1)S(1)}, bf16[1,3,3,512,512]{4,3,2,1,0:T(8,128)(2,1)}, u32[]{:S(2)}) copy-start(bf16[1,3,3,512,512]{4,3,2,1,0:T(8,128)(2,1)} %param.12) | copy-start | bytes 14155780
  7.6 7.4 %collective-permute-start = (bf16[2,32,512]{2,1,0:T(8,128)(2,1)S(1)}, bf16[2,32,512]{2,1,0:T(8,128)(2,1)S(1)}, u32[]{:S(2)}, u32[]{:S(2)}) collective-permute-start(bf16[2,32,512]{2,1,0:T(8,128)(2,1)S(1)} %get-tuple-element.11), channel_id=1, source_target_pairs={{0,1},{1,2},{2,3},{3,4},{4,5},{5,6},{6,7},{7,8},{8,9},{9,10},{10,1... | collective-permute-start | bytes 196616 | tf_op jit(solution)/shard_map/ppermute | solution.py:15
  13.0 6.8 %collective-permute-start.1 = (bf16[2,32,512]{2,1,0:T(8,128)(2,1)S(1)}, bf16[2,32,512]{2,1,0:T(8,128)(2,1)S(1)}, u32[]{:S(2)}, u32[]{:S(2)}) collective-permute-start(bf16[2,32,512]{2,1,0:T(8,128)(2,1)S(1)} %get-tuple-element.12), channel_id=1, source_target_pairs={{1,0},{2,1},{3,2},{4,3},{5,4},{6,5},{7,6},{8,7},{9,8},{10,9},{11,1... | collective-permute-start | bytes 196616 | tf_op jit(solution)/shard_map/ppermute | solution.py:17
  24.3 1.4 copy-start.1
  25.7 1.4 copy-start.4
  25.7 1.4 copy-start.6
  26.6 11.2 %slice-start = ((s8[4718592]{0:T(1024)(128)(4,1)}), s8[4194304]{0:T(1024)(128)(4,1)S(1)}, s32[]{:S(2)}) async-start(s8[4718592]{0:T(1024)(128)(4,1)} %bitcast.142), calls=%async_computation.1 | async-start | bytes 8388608
  27.1 10.7 %slice-start.1 = ((s8[4718592]{0:T(1024)(128)(4,1)}), s8[524288]{0:T(1024)(128)(4,1)S(1)}, s32[]{:S(2)}) async-start(s8[4718592]{0:T(1024)(128)(4,1)} %bitcast.142), calls=%async_computation.2 | async-start | bytes 1048576
  27.8 4.5 %collective-permute-start.2 = (bf16[4,32,512]{2,1,0:T(8,128)(2,1)S(1)}, bf16[4,32,512]{2,1,0:T(8,128)(2,1)S(1)}, u32[]{:S(2)}, u32[]{:S(2)}) collective-permute-start(bf16[4,32,512]{2,1,0:T(8,128)(2,1)S(1)} %get-tuple-element.9), channel_id=1, source_target_pairs={{0,1},{1,2},{2,3},{3,4},{4,5},{5,6},{6,7},{7,8},{8,9},{9,10},{10,1... | collective-permute-start | bytes 393224 | tf_op jit(solution)/shard_map/ppermute | solution.py:15
  29.9 7.5 %collective-permute-start.3 = (bf16[4,32,512]{2,1,0:T(8,128)(2,1)S(1)}, bf16[4,32,512]{2,1,0:T(8,128)(2,1)S(1)}, u32[]{:S(2)}, u32[]{:S(2)}) collective-permute-start(bf16[4,32,512]{2,1,0:T(8,128)(2,1)S(1)} %get-tuple-element.10), channel_id=1, source_target_pairs={{1,0},{2,1},{3,2},{4,3},{5,4},{6,5},{7,6},{8,7},{9,8},{10,9},{11,1... | collective-permute-start | bytes 393224 | tf_op jit(solution)/shard_map/ppermute | solution.py:17
  40.0 1.4 copy-start.3
  40.1 1.4 copy-start.5
  41.4 1.5 copy-start.7
  41.4 96.6 %slice-start.2 = ((s8[4718592]{0:T(1024)(128)(4,1)}), s8[524288]{0:T(1024)(128)(4,1)S(1)}, s32[]{:S(2)}) async-start(s8[4718592]{0:T(1024)(128)(4,1)} %bitcast.153), calls=%async_computation.3 | async-start | bytes 1048576
  42.9 80.8 %copy-start.2 = (bf16[1,16,32,512]{3,2,1,0:T(8,128)(2,1)S(1)}, bf16[1,16,32,512]{3,2,1,0:T(8,128)(2,1)}, u32[]{:S(2)}) copy-start(bf16[1,16,32,512]{3,2,1,0:T(8,128)(2,1)} %param.10) | copy-start | bytes 1572868
  117.9 20.2 %slice-start.3 = ((s8[4718592]{0:T(1024)(128)(4,1)}), s8[4194304]{0:T(1024)(128)(4,1)S(1)}, s32[]{:S(2)}) async-start(s8[4718592]{0:T(1024)(128)(4,1)} %bitcast.153), calls=%async_computation.4 | async-start | bytes 8388608
  124.4 7.8 %collective-permute-start.4 = (bf16[4,32,512]{2,1,0:T(8,128)(2,1)S(1)}, bf16[4,32,512]{2,1,0:T(8,128)(2,1)S(1)}, u32[]{:S(2)}, u32[]{:S(2)}) collective-permute-start(bf16[4,32,512]{2,1,0:T(8,128)(2,1)S(1)} %get-tuple-element.7), channel_id=1, source_target_pairs={{0,1},{1,2},{2,3},{3,4},{4,5},{5,6},{6,7},{7,8},{8,9},{9,10},{10,1... | collective-permute-start | bytes 393224 | tf_op jit(solution)/shard_map/ppermute | solution.py:15
  130.0 7.5 %collective-permute-start.5 = (bf16[4,32,512]{2,1,0:T(8,128)(2,1)S(1)}, bf16[4,32,512]{2,1,0:T(8,128)(2,1)S(1)}, u32[]{:S(2)}, u32[]{:S(2)}) collective-permute-start(bf16[4,32,512]{2,1,0:T(8,128)(2,1)S(1)} %get-tuple-element.8), channel_id=1, source_target_pairs={{1,0},{2,1},{3,2},{4,3},{5,4},{6,5},{7,6},{8,7},{9,8},{10,9},{11,1... | collective-permute-start | bytes 393224 | tf_op jit(solution)/shard_map/ppermute | solution.py:17
  141.4 10.5 %slice-start.4 = ((s8[4718592]{0:T(1024)(128)(4,1)}), s8[524288]{0:T(1024)(128)(4,1)S(1)}, s32[]{:S(2)}) async-start(s8[4718592]{0:T(1024)(128)(4,1)} %bitcast.173), calls=%async_computation.5 | async-start | bytes 1048576
  141.9 10.0 %slice-start.5 = ((s8[4718592]{0:T(1024)(128)(4,1)}), s8[4194304]{0:T(1024)(128)(4,1)S(1)}, s32[]{:S(2)}) async-start(s8[4718592]{0:T(1024)(128)(4,1)} %bitcast.173), calls=%async_computation.6 | async-start | bytes 8388608
  142.6 4.5 %collective-permute-start.6 = (bf16[2,32,512]{2,1,0:T(8,128)(2,1)S(1)}, bf16[2,32,512]{2,1,0:T(8,128)(2,1)S(1)}, u32[]{:S(2)}, u32[]{:S(2)}) collective-permute-start(bf16[2,32,512]{2,1,0:T(8,128)(2,1)S(1)} %get-tuple-element.5), channel_id=1, source_target_pairs={{0,1},{1,2},{2,3},{3,4},{4,5},{5,6},{6,7},{7,8},{8,9},{9,10},{10,1... | collective-permute-start | bytes 196616 | tf_op jit(solution)/shard_map/ppermute | solution.py:15
  144.7 6.8 %collective-permute-start.7 = (bf16[2,32,512]{2,1,0:T(8,128)(2,1)S(1)}, bf16[2,32,512]{2,1,0:T(8,128)(2,1)S(1)}, u32[]{:S(2)}, u32[]{:S(2)}) collective-permute-start(bf16[2,32,512]{2,1,0:T(8,128)(2,1)S(1)} %get-tuple-element.6), channel_id=1, source_target_pairs={{1,0},{2,1},{3,2},{4,3},{5,4},{6,5},{7,6},{8,7},{9,8},{10,9},{11,1... | collective-permute-start | bytes 196616 | tf_op jit(solution)/shard_map/ppermute | solution.py:17
Sparse Core Ops, SparseCore 0:
  43.1 74.7 all-gather.2
where the time goes:
time: 164 us
  waiting for transfers between devices  94 us (57%)
  matrix products  26.8 us (16%)
  starting transfers between devices  24.1 us (15%)
  between operations  14 us (9%)
  other arithmetic  3.18 us (2%)
  local copies, waits for them, and re-layouts  1.76 us (1%)
    all_gather x1, waiting for transfers between devices, per_device(): piece = lax.all_gather(feat[None], 'peer', axis=0, tiled=True)  74.3 us
    ppermute x4, waiting for transfers between devices, extended(): lax.ppermute(head, axis, [((i + 1) % count, i) for i in range(ends)])  19.7 us
    ppermute x4, starting transfers between devices, extended(): lax.ppermute(tail, axis, [(i, (i + 1) % count) for i in range(ends)])  15.2 us
    dot_general x18, matrix products, apply_dilated_filter(): jnp.einsum('rwi,io->rwo', input_window, filter_kernel[kernel_tap_row, ker...  11.4 us
    dot_general x18, matrix products, apply_dilated_filter(): jnp.einsum('rwo,io->rwi', input_window, filter_kernel[2 - kernel_tap_row,...  9.54 us
    ppermute x4, starting transfers between devices, extended(): lax.ppermute(head, axis, [((i + 1) % count, i) for i in range(ends)])  8.83 us
    dot_general x1, matrix products, per_device(): jnp.einsum('k,krwc->rwc', pick, piece, preferred_element_type=jnp.float32)  5.87 us
  transfers between devices with their start and end apart: 9, of which 5 were waited for; matrix products, arithmetic and copies ran while one was open for 0% of the time, Pallas kernels for 0%

commit v1 on v0

--- a/solution.py
+++ b/solution.py
@@ -85,7 +85,10 @@
     )
     feat = jax.nn.silu(pre_second).astype(jnp.bfloat16)
     partner = pairing[lax.axis_index("peer")]
-    piece = lax.all_gather(feat[None], "peer", axis=0, tiled=True)
+    vals = feat[None]
+    piece = jnp.concatenate(
+        lax.all_to_all(jnp.stack(lax.axis_size("peer") * [vals]), "peer", 0, 0), axis=0
+    )
     owners = jnp.arange(piece.shape[0], dtype=jnp.int32)
     pick = (owners == partner).astype(jnp.bfloat16)
     partner_feat = jnp.einsum("k,krwc->rwc", pick, piece, preferred_element_type=jnp.float32)

time: 164 us -> 139 us (0.85)
  waiting for transfers between devices: 94 us -> 76.8 us
  between operations: 14 us -> 0.59 us
  starting transfers between devices: 24.1 us -> 28.1 us
  local copies, waits for them, and re-layouts: 1.76 us -> 4.29 us
    all_gather x1 -> x0, waiting for transfers between devices: 74.3 us -> none  [per_device(): piece = lax.all_gather(feat[None], 'peer', axis=0, tiled=True)]
    all_to_all x0 -> x1, waiting for transfers between devices: none -> 57.2 us  [per_device(): lax.all_to_all(jnp.stack(lax.axis_size('peer') * [vals]), 'peer', 0, 0)]
    all_to_all x0 -> x1, starting transfers between devices: none -> 6.78 us  [per_device(): lax.all_to_all(jnp.stack(lax.axis_size('peer') * [vals]), 'peer', 0, 0)]
    ppermute x4, starting transfers between devices: 15.2 us -> 12.5 us  [extended(): lax.ppermute(tail, axis, [(i, (i + 1) % count) for i in range(ends)])]
    another operation x0 -> x1, local copies, waits for them, and re-layouts: none -> 2.54 us  [per_device(): jnp.stack(lax.axis_size('peer') * [vals])]
where the time goes in v1:
time: 139 us
  waiting for transfers between devices  76.8 us (55%)
  starting transfers between devices  28.1 us (20%)
  matrix products  26 us (19%)
  local copies, waits for them, and re-layouts  4.29 us (3%)
  other arithmetic  3.18 us (2%)
    all_to_all x1, waiting for transfers between devices, per_device(): lax.all_to_all(jnp.stack(lax.axis_size('peer') * [vals]), 'peer', 0, 0)  57.2 us
    ppermute x4, waiting for transfers between devices, extended(): lax.ppermute(head, axis, [((i + 1) % count, i) for i in range(ends)])  19.7 us
    ppermute x4, starting transfers between devices, extended(): lax.ppermute(tail, axis, [(i, (i + 1) % count) for i in range(ends)])  12.5 us
    dot_general x18, matrix products, apply_dilated_filter(): jnp.einsum('rwi,io->rwo', input_window, filter_kernel[kernel_tap_row, ker...  10.6 us
    dot_general x18, matrix products, apply_dilated_filter(): jnp.einsum('rwo,io->rwi', input_window, filter_kernel[2 - kernel_tap_row,...  9.55 us
    ppermute x4, starting transfers between devices, extended(): lax.ppermute(head, axis, [((i + 1) % count, i) for i in range(ends)])  8.83 us
    all_to_all x1, starting transfers between devices, per_device(): lax.all_to_all(jnp.stack(lax.axis_size('peer') * [vals]), 'peer', 0, 0)  6.78 us
    dot_general x1, matrix products, per_device(): jnp.einsum('k,krwc->rwc', pick, piece, preferred_element_type=jnp.float32)  5.9 us
  transfers between devices with their start and end apart: 9, of which 5 were waited for; matrix products, arithmetic and copies ran while one was open for 0% of the time, Pallas kernels for 0%

profile of v1, /device:TPU:97, one launch (start us, length us, event | category | flops | bytes accessed | tf_op | source)
XLA Modules:
  0.0 139.0 jit_solution(1108909621203328763)
XLA Ops:
  0.0 1.0 slice_bitcast_fusion.55
  1.0 5.4 %collective-permute-start = (bf16[2,32,512]{2,1,0:T(8,128)(2,1)S(1)}, bf16[2,32,512]{2,1,0:T(8,128)(2,1)S(1)}, u32[]{:S(2)}, u32[]{:S(2)}) collective-permute-start(bf16[2,32,512]{2,1,0:T(8,128)(2,1)S(1)} %get-tuple-element.11), channel_id=1, source_target_pairs={{0,1},{1,2},{2,3},{3,4},{4,5},{5,6},{6,7},{7,8},{8,9},{9,10},{10,1... | collective-permute-start | bytes 196616 | tf_op jit(solution)/shard_map/ppermute | solution.py:15
  6.5 1.9 %collective-permute-start.1 = (bf16[2,32,512]{2,1,0:T(8,128)(2,1)S(1)}, bf16[2,32,512]{2,1,0:T(8,128)(2,1)S(1)}, u32[]{:S(2)}, u32[]{:S(2)}) collective-permute-start(bf16[2,32,512]{2,1,0:T(8,128)(2,1)S(1)} %get-tuple-element.12), channel_id=1, source_target_pairs={{1,0},{2,1},{3,2},{4,3},{5,4},{6,5},{7,6},{8,7},{9,8},{10,9},{11,1... | collective-permute-start | bytes 196616 | tf_op jit(solution)/shard_map/ppermute | solution.py:17
  8.4 4.9 %collective-permute-done.1 = bf16[2,32,512]{2,1,0:T(8,128)(2,1)S(1)} collective-permute-done((bf16[2,32,512]{2,1,0:T(8,128)(2,1)S(1)}, bf16[2,32,512]{2,1,0:T(8,128)(2,1)S(1)}, u32[]{:S(2)}, u32[]{:S(2)}) %collective-permute-start.1) | collective-permute-done | bytes 65568 | tf_op jit(solution)/shard_map/ppermute | solution.py:17
  13.3 1.4 fusion.30
  14.7 1.5 %fusion.80 = f32[16,32,512]{2,1,0:T(8,128)S(1)} fusion(bf16[20,36,512]{2,1,0:T(8,128)(2,1)S(1)} %fusion.30, bf16[3,3,512,512]{3,2,1,0:T(8,128)(2,1)} %bitcast.164), kind=kOutput, calls=%fused_computation.131 | convolution fusion | flops 268435456 | bytes 2097152 | tf_op jit(solution)/shard_map/rwi,io->rwo/dot_general | solution.py:44
  16.1 1.6 %fusion.45 = f32[16,32,512]{2,1,0:T(8,128)S(1)} fusion(bf16[16,32,512]{2,1,0:T(8,128)(2,1)} %bitcast.185, bf16[2,32,512]{2,1,0:T(8,128)(2,1)S(1)} %collective-permute-done, bf16[3,3,512,512]{3,2,1,0:T(8,128)(2,1)} %bitcast.165), kind=kOutput, calls=%fused_computation.86 | convolution fusion | flops 269615104 | bytes 2162688 | tf_op jit(solution)/shard_map/rwi,io->rwo/dot_general | solution.py:44
  20.6 0.7 multiply_convert_fusion.1
  21.3 2.1 %collective-permute-start.2 = (bf16[4,32,512]{2,1,0:T(8,128)(2,1)S(1)}, bf16[4,32,512]{2,1,0:T(8,128)(2,1)S(1)}, u32[]{:S(2)}, u32[]{:S(2)}) collective-permute-start(bf16[4,32,512]{2,1,0:T(8,128)(2,1)S(1)} %get-tuple-element.9), channel_id=1, source_target_pairs={{0,1},{1,2},{2,3},{3,4},{4,5},{5,6},{6,7},{7,8},{8,9},{9,10},{10,1... | collective-permute-start | bytes 393224 | tf_op jit(solution)/shard_map/ppermute | solution.py:15
  23.3 2.4 %collective-permute-start.3 = (bf16[4,32,512]{2,1,0:T(8,128)(2,1)S(1)}, bf16[4,32,512]{2,1,0:T(8,128)(2,1)S(1)}, u32[]{:S(2)}, u32[]{:S(2)}) collective-permute-start(bf16[4,32,512]{2,1,0:T(8,128)(2,1)S(1)} %get-tuple-element.10), channel_id=1, source_target_pairs={{1,0},{2,1},{3,2},{4,3},{5,4},{6,5},{7,6},{8,7},{9,8},{10,9},{11,1... | collective-permute-start | bytes 393224 | tf_op jit(solution)/shard_map/ppermute | solution.py:17
  25.7 5.1 %collective-permute-done.3 = bf16[4,32,512]{2,1,0:T(8,128)(2,1)S(1)} collective-permute-done((bf16[4,32,512]{2,1,0:T(8,128)(2,1)S(1)}, bf16[4,32,512]{2,1,0:T(8,128)(2,1)S(1)}, u32[]{:S(2)}, u32[]{:S(2)}) %collective-permute-start.3) | collective-permute-done | bytes 131104 | tf_op jit(solution)/shard_map/ppermute | solution.py:17
  34.9 0.7 multiply_convert_fusion
  35.6 2.5 %stack.3 = bf16[8,1,16,32,512]{4,3,2,1,0:T(8,128)(2,1)} broadcast(bf16[16,32,512]{2,1,0:T(8,128)(2,1)S(1)} %get-tuple-element.15), dimensions={2,3,4} | broadcast | bytes 4718592 | tf_op jit(solution)/shard_map/stack | solution.py:90
  38.1 6.8 %all-to-all-start = ((bf16[8,1,16,32,512]{4,3,2,1,0:T(8,128)(2,1)}), bf16[8,1,16,32,512]{4,3,2,1,0:T(8,128)(2,1)}, u32[]{:S(2)}, u32[]{:S(2)}) async-start(bf16[8,1,16,32,512]{4,3,2,1,0:T(8,128)(2,1)} %stack.3), calls=%async_computation | async-start | bytes 8388608 | tf_op jit(solution)/shard_map/all_to_all | solution.py:90
  45.5 57.2 %all-to-all-done = bf16[8,1,16,32,512]{4,3,2,1,0:T(8,128)(2,1)} async-done(((bf16[8,1,16,32,512]{4,3,2,1,0:T(8,128)(2,1)}), bf16[8,1,16,32,512]{4,3,2,1,0:T(8,128)(2,1)}, u32[]{:S(2)}, u32[]{:S(2)}) %all-to-all-start) | async-done | bytes 4194336 | tf_op jit(solution)/shard_map/all_to_all | solution.py:90
  102.7 5.9 %fusion = f32[1,16,32,512]{3,0,2,1:T(1,128)S(1)} fusion(bf16[8,16,32,512]{3,2,1,0:T(8,128)(2,1)} %bitcast.49, s32[]{:T(128)} %bitcast.46), kind=kOutput, calls=%fused_computation | convolution fusion | flops 4194312 | bytes 5242884 | tf_op jit(solution)/shard_map/k,krwc->rwc/dot_general | solution.py:94
  109.2 2.9 %collective-permute-start.4 = (bf16[4,32,512]{2,1,0:T(8,128)(2,1)S(1)}, bf16[4,32,512]{2,1,0:T(8,128)(2,1)S(1)}, u32[]{:S(2)}, u32[]{:S(2)}) collective-permute-start(bf16[4,32,512]{2,1,0:T(8,128)(2,1)S(1)} %get-tuple-element.7), channel_id=1, source_target_pairs={{0,1},{1,2},{2,3},{3,4},{4,5},{5,6},{6,7},{7,8},{8,9},{9,10},{10,1... | collective-permute-start | bytes 393224 | tf_op jit(solution)/shard_map/ppermute | solution.py:15
  112.1 2.1 %collective-permute-start.5 = (bf16[4,32,512]{2,1,0:T(8,128)(2,1)S(1)}, bf16[4,32,512]{2,1,0:T(8,128)(2,1)S(1)}, u32[]{:S(2)}, u32[]{:S(2)}) collective-permute-start(bf16[4,32,512]{2,1,0:T(8,128)(2,1)S(1)} %get-tuple-element.8), channel_id=1, source_target_pairs={{1,0},{2,1},{3,2},{4,3},{5,4},{6,5},{7,6},{8,7},{9,8},{10,9},{11,1... | collective-permute-start | bytes 393224 | tf_op jit(solution)/shard_map/ppermute | solution.py:17
  114.2 5.4 %collective-permute-done.5 = bf16[4,32,512]{2,1,0:T(8,128)(2,1)S(1)} collective-permute-done((bf16[4,32,512]{2,1,0:T(8,128)(2,1)S(1)}, bf16[4,32,512]{2,1,0:T(8,128)(2,1)S(1)}, u32[]{:S(2)}, u32[]{:S(2)}) %collective-permute-start.5) | collective-permute-done | bytes 131104 | tf_op jit(solution)/shard_map/ppermute | solution.py:17
  123.9 0.7 fusion.15
  124.7 2.1 %collective-permute-start.6 = (bf16[2,32,512]{2,1,0:T(8,128)(2,1)S(1)}, bf16[2,32,512]{2,1,0:T(8,128)(2,1)S(1)}, u32[]{:S(2)}, u32[]{:S(2)}) collective-permute-start(bf16[2,32,512]{2,1,0:T(8,128)(2,1)S(1)} %get-tuple-element.5), channel_id=1, source_target_pairs={{0,1},{1,2},{2,3},{3,4},{4,5},{5,6},{6,7},{7,8},{8,9},{9,10},{10,1... | collective-permute-start | bytes 196616 | tf_op jit(solution)/shard_map/ppermute | solution.py:15
  126.7 2.4 %collective-permute-start.7 = (bf16[2,32,512]{2,1,0:T(8,128)(2,1)S(1)}, bf16[2,32,512]{2,1,0:T(8,128)(2,1)S(1)}, u32[]{:S(2)}, u32[]{:S(2)}) collective-permute-start(bf16[2,32,512]{2,1,0:T(8,128)(2,1)S(1)} %get-tuple-element.6), channel_id=1, source_target_pairs={{1,0},{2,1},{3,2},{4,3},{5,4},{6,5},{7,6},{8,7},{9,8},{10,9},{11,1... | collective-permute-start | bytes 196616 | tf_op jit(solution)/shard_map/ppermute | solution.py:17
  129.2 4.4 %collective-permute-done.7 = bf16[2,32,512]{2,1,0:T(8,128)(2,1)S(1)} collective-permute-done((bf16[2,32,512]{2,1,0:T(8,128)(2,1)S(1)}, bf16[2,32,512]{2,1,0:T(8,128)(2,1)S(1)}, u32[]{:S(2)}, u32[]{:S(2)}) %collective-permute-start.7) | collective-permute-done | bytes 65568 | tf_op jit(solution)/shard_map/ppermute | solution.py:17
  137.7 1.3 fusion.16
  (73 shorter events, 16.2 us)
Async XLA Ops:
  0.0 17.8 %copy-start = (bf16[1,3,3,512,512]{4,3,2,1,0:T(8,128)(2,1)S(1)}, bf16[1,3,3,512,512]{4,3,2,1,0:T(8,128)(2,1)}, u32[]{:S(2)}) copy-start(bf16[1,3,3,512,512]{4,3,2,1,0:T(8,128)(2,1)} %param.12) | copy-start | bytes 14155780
  1.0 7.4 %collective-permute-start = (bf16[2,32,512]{2,1,0:T(8,128)(2,1)S(1)}, bf16[2,32,512]{2,1,0:T(8,128)(2,1)S(1)}, u32[]{:S(2)}, u32[]{:S(2)}) collective-permute-start(bf16[2,32,512]{2,1,0:T(8,128)(2,1)S(1)} %get-tuple-element.11), channel_id=1, source_target_pairs={{0,1},{1,2},{2,3},{3,4},{4,5},{5,6},{6,7},{7,8},{8,9},{9,10},{10,1... | collective-permute-start | bytes 196616 | tf_op jit(solution)/shard_map/ppermute | solution.py:15
  6.5 6.8 %collective-permute-start.1 = (bf16[2,32,512]{2,1,0:T(8,128)(2,1)S(1)}, bf16[2,32,512]{2,1,0:T(8,128)(2,1)S(1)}, u32[]{:S(2)}, u32[]{:S(2)}) collective-permute-start(bf16[2,32,512]{2,1,0:T(8,128)(2,1)S(1)} %get-tuple-element.12), channel_id=1, source_target_pairs={{1,0},{2,1},{3,2},{4,3},{5,4},{6,5},{7,6},{8,7},{9,8},{10,9},{11,1... | collective-permute-start | bytes 196616 | tf_op jit(solution)/shard_map/ppermute | solution.py:17
  17.8 1.4 copy-start.1
  19.1 1.4 %copy-start.4 = (f32[1,512]{1,0:T(1,128)S(1)}, f32[1,512]{1,0:T(1,128)}, u32[]{:S(2)}) copy-start(f32[1,512]{1,0:T(1,128)} %param.14) | copy-start | bytes 6148
  19.2 1.4 copy-start.6
  20.1 11.2 %slice-start = ((s8[4718592]{0:T(1024)(128)(4,1)}), s8[4194304]{0:T(1024)(128)(4,1)S(1)}, s32[]{:S(2)}) async-start(s8[4718592]{0:T(1024)(128)(4,1)} %bitcast.142), calls=%async_computation.1 | async-start | bytes 8388608
  20.5 10.7 %slice-start.1 = ((s8[4718592]{0:T(1024)(128)(4,1)}), s8[524288]{0:T(1024)(128)(4,1)S(1)}, s32[]{:S(2)}) async-start(s8[4718592]{0:T(1024)(128)(4,1)} %bitcast.142), calls=%async_computation.2 | async-start | bytes 1048576
  21.3 4.5 %collective-permute-start.2 = (bf16[4,32,512]{2,1,0:T(8,128)(2,1)S(1)}, bf16[4,32,512]{2,1,0:T(8,128)(2,1)S(1)}, u32[]{:S(2)}, u32[]{:S(2)}) collective-permute-start(bf16[4,32,512]{2,1,0:T(8,128)(2,1)S(1)} %get-tuple-element.9), channel_id=1, source_target_pairs={{0,1},{1,2},{2,3},{3,4},{4,5},{5,6},{6,7},{7,8},{8,9},{9,10},{10,1... | collective-permute-start | bytes 393224 | tf_op jit(solution)/shard_map/ppermute | solution.py:15
  23.3 7.5 %collective-permute-start.3 = (bf16[4,32,512]{2,1,0:T(8,128)(2,1)S(1)}, bf16[4,32,512]{2,1,0:T(8,128)(2,1)S(1)}, u32[]{:S(2)}, u32[]{:S(2)}) collective-permute-start(bf16[4,32,512]{2,1,0:T(8,128)(2,1)S(1)} %get-tuple-element.10), channel_id=1, source_target_pairs={{1,0},{2,1},{3,2},{4,3},{5,4},{6,5},{7,6},{8,7},{9,8},{10,9},{11,1... | collective-permute-start | bytes 393224 | tf_op jit(solution)/shard_map/ppermute | solution.py:17
  33.5 1.4 copy-start.3
  33.5 1.4 copy-start.5
  38.1 6.8 %copy-start.7 = (s32[8]{0:T(128)S(1)}, s32[8]{0:T(128)}, u32[]{:S(2)}) copy-start(s32[8]{0:T(128)} %param.11) | copy-start | bytes 100
  38.1 82.0 %slice-start.2 = ((s8[4718592]{0:T(1024)(128)(4,1)}), s8[524288]{0:T(1024)(128)(4,1)S(1)}, s32[]{:S(2)}) async-start(s8[4718592]{0:T(1024)(128)(4,1)} %bitcast.153), calls=%async_computation.3 | async-start | bytes 1048576
  38.1 64.5 %all-to-all-start = ((bf16[8,1,16,32,512]{4,3,2,1,0:T(8,128)(2,1)}), bf16[8,1,16,32,512]{4,3,2,1,0:T(8,128)(2,1)}, u32[]{:S(2)}, u32[]{:S(2)}) async-start(bf16[8,1,16,32,512]{4,3,2,1,0:T(8,128)(2,1)} %stack.3), calls=%async_computation | async-start | bytes 8388608 | tf_op jit(solution)/shard_map/all_to_all | solution.py:90
  44.9 63.7 %copy-start.2 = (bf16[1,16,32,512]{3,2,1,0:T(8,128)(2,1)S(1)}, bf16[1,16,32,512]{3,2,1,0:T(8,128)(2,1)}, u32[]{:S(2)}) copy-start(bf16[1,16,32,512]{3,2,1,0:T(8,128)(2,1)} %param.10) | copy-start | bytes 1572868
  102.6 17.4 %slice-start.3 = ((s8[4718592]{0:T(1024)(128)(4,1)}), s8[4194304]{0:T(1024)(128)(4,1)S(1)}, s32[]{:S(2)}) async-start(s8[4718592]{0:T(1024)(128)(4,1)} %bitcast.153), calls=%async_computation.4 | async-start | bytes 8388608
  109.2 5.0 %collective-permute-start.4 = (bf16[4,32,512]{2,1,0:T(8,128)(2,1)S(1)}, bf16[4,32,512]{2,1,0:T(8,128)(2,1)S(1)}, u32[]{:S(2)}, u32[]{:S(2)}) collective-permute-start(bf16[4,32,512]{2,1,0:T(8,128)(2,1)S(1)} %get-tuple-element.7), channel_id=1, source_target_pairs={{0,1},{1,2},{2,3},{3,4},{4,5},{5,6},{6,7},{7,8},{8,9},{9,10},{10,1... | collective-permute-start | bytes 393224 | tf_op jit(solution)/shard_map/ppermute | solution.py:15
  112.1 7.5 %collective-permute-start.5 = (bf16[4,32,512]{2,1,0:T(8,128)(2,1)S(1)}, bf16[4,32,512]{2,1,0:T(8,128)(2,1)S(1)}, u32[]{:S(2)}, u32[]{:S(2)}) collective-permute-start(bf16[4,32,512]{2,1,0:T(8,128)(2,1)S(1)} %get-tuple-element.8), channel_id=1, source_target_pairs={{1,0},{2,1},{3,2},{4,3},{5,4},{6,5},{7,6},{8,7},{9,8},{10,9},{11,1... | collective-permute-start | bytes 393224 | tf_op jit(solution)/shard_map/ppermute | solution.py:17
  123.4 10.5 %slice-start.4 = ((s8[4718592]{0:T(1024)(128)(4,1)}), s8[4194304]{0:T(1024)(128)(4,1)S(1)}, s32[]{:S(2)}) async-start(s8[4718592]{0:T(1024)(128)(4,1)} %bitcast.173), calls=%async_computation.5 | async-start | bytes 8388608
  123.9 10.0 %slice-start.5 = ((s8[4718592]{0:T(1024)(128)(4,1)}), s8[524288]{0:T(1024)(128)(4,1)S(1)}, s32[]{:S(2)}) async-start(s8[4718592]{0:T(1024)(128)(4,1)} %bitcast.173), calls=%async_computation.6 | async-start | bytes 1048576
  124.7 4.5 %collective-permute-start.6 = (bf16[2,32,512]{2,1,0:T(8,128)(2,1)S(1)}, bf16[2,32,512]{2,1,0:T(8,128)(2,1)S(1)}, u32[]{:S(2)}, u32[]{:S(2)}) collective-permute-start(bf16[2,32,512]{2,1,0:T(8,128)(2,1)S(1)} %get-tuple-element.5), channel_id=1, source_target_pairs={{0,1},{1,2},{2,3},{3,4},{4,5},{5,6},{6,7},{7,8},{8,9},{9,10},{10,1... | collective-permute-start | bytes 196616 | tf_op jit(solution)/shard_map/ppermute | solution.py:15
  126.7 6.8 %collective-permute-start.7 = (bf16[2,32,512]{2,1,0:T(8,128)(2,1)S(1)}, bf16[2,32,512]{2,1,0:T(8,128)(2,1)S(1)}, u32[]{:S(2)}, u32[]{:S(2)}) collective-permute-start(bf16[2,32,512]{2,1,0:T(8,128)(2,1)S(1)} %get-tuple-element.6), channel_id=1, source_target_pairs={{1,0},{2,1},{3,2},{4,3},{5,4},{6,5},{7,6},{8,7},{9,8},{10,9},{11,1... | collective-permute-start | bytes 196616 | tf_op jit(solution)/shard_map/ppermute | solution.py:17
